TPU v7x, 128 devices: a whole 4x4x4 slice. The times are simulated.
128 devices in a mesh: fx: 8 (over y_hi, z), fy: 16 (over x, y_lo, core).
Axes of the slice: x: 4, y: 4 (y_hi: 2, y_lo: 2; y = y_hi * 2 + y_lo), z: 4, core: 2. Of those that a mesh axis runs over, the one named last changes fastest.
Arguments:
- facets: float32 [8192, 4096], P('fx', 'fy'), may hold values from -6 to 6
- counts: int32 [8, 16], P('fx', 'fy'), may hold values from 1 to 16, as said below
- cells: int32 [2, 8, 16, 2048], P(None, 'fx', 'fy'), may hold values from 0 to 248
- fracs: float32 [2, 8, 16, 2048], P(None, 'fx', 'fy'), may hold values from 0 to 1
Outputs:
- predictions: float32 [2, 8, 16, 2048], P(None, 'fx', 'fy')
Inputs may be any that keep to these rules, and one draw needn't show every extreme that they name: Blocks 0 to counts - 1 of a subgrid's 128-visibility blocks are live, the others are padding; some subgrid has 16 live blocks.
All inputs are finite; a program needn't handle non-finite values.
Results may differ from a plain program's by a relative error of at most 0.0003.
Values sent between devices are 32-bit elements; how exact they have to be, the bound alone decides.
A program may use at most 128 MiB of HBM per device.

v0:
```python
import math
import jax
import jax.numpy as jnp
from jax import lax
from jax.sharding import Mesh
from jax.sharding import PartitionSpec as P

NIMG = 65536
FP = 4096
SUBGRID = 256
SUPPORT = 8
VBLOCK = 128
FX = ("fx_0", "fx_1")


def sum_in_order(blocks, axes, turns):
    dims = [lax.axis_size(a) for a in axes]
    blocks = blocks.reshape(*dims, *blocks.shape[1:])
    blocks = blocks.transpose(*turns, *range(len(axes), blocks.ndim))
    blocks = blocks.reshape(-1, *blocks.shape[len(axes) :])
    for k in turns:
        blocks = lax.psum_scatter(blocks, axes[k], scatter_dimension=0, tiled=True)
    return blocks[0]


def split_up(array, dim, length):
    before, after = (array.shape[:dim], array.shape[dim + 1 :])
    return jnp.moveaxis(array.reshape(*before, length, -1, *after), dim, 0)


def summed_rows(array, axes, turns, dim):
    length = lax.axis_size(axes)
    return sum_in_order(split_up(array, dim, length), axes, turns)


def mulmod(upper, lower):
    low = upper % 256
    high = upper // 256
    return (low * lower + 256 * (high * lower % (NIMG // 256))) % NIMG


def factor(freqs, pixels, scale):
    inner = pixels % FP
    turns = mulmod(freqs[:, None], pixels[None, :])
    angle = turns.astype(jnp.float32) * (2.0 * math.pi / NIMG)
    window = jnp.sin(math.pi * (inner.astype(jnp.float32) + 0.5) / FP) * scale
    return (jnp.cos(angle) * window[None, :], -jnp.sin(angle) * window[None, :])


def kernel(offset, frac):
    positions = jnp.arange(SUBGRID, dtype=jnp.int32)
    dist = positions[None, :] - offset[:, None]
    inside = (dist >= 0) & (dist < SUPPORT)
    shift = dist.astype(jnp.float32) - (SUPPORT // 2 - 1) - frac[:, None]
    value = 0.6 * jnp.exp(-shift * shift / 4.5)
    return jnp.where(inside, value, jnp.zeros_like(value))


def column_term(v_start, v_count, p_real, p_imag, columns, scale):
    freqs = v_start * SUBGRID + jnp.arange(v_count * SUBGRID, dtype=jnp.int32)
    b_real, b_imag = factor(freqs, columns, scale)
    left = jnp.concatenate([b_real, b_imag], axis=0)
    right = jnp.concatenate([p_real, p_imag], axis=0)
    product = lax.dot_general(
        left,
        right,
        (((1,), (1,)), ((), ())),
        precision=lax.Precision.HIGHEST,
        preferred_element_type=jnp.float32,
    )
    height = v_count * SUBGRID
    width = p_real.shape[0]
    t_real = product[:height, :width] - product[height:, width:]
    t_imag = product[height:, :width] + product[:height, width:]
    return jnp.stack(
        [t_real.reshape(v_count, SUBGRID, width), t_imag.reshape(v_count, SUBGRID, width)], axis=1
    )


def degrid(values, grid, cell_rows, frac_rows, row, col, stride, turns):
    highest = lax.Precision.HIGHEST

    def step(turn, values):
        offset = stride * turn * VBLOCK
        cells_u = lax.dynamic_slice_in_dim(cell_rows[0], offset, VBLOCK)
        cells_v = lax.dynamic_slice_in_dim(cell_rows[1], offset, VBLOCK)
        fracs_u = lax.dynamic_slice_in_dim(frac_rows[0], offset, VBLOCK)
        fracs_v = lax.dynamic_slice_in_dim(frac_rows[1], offset, VBLOCK)
        weight_u = kernel(cells_u, fracs_u)
        weight_v = kernel(cells_v, fracs_v)
        g_real = jnp.dot(weight_v, grid[0], precision=highest, preferred_element_type=jnp.float32)
        g_imag = jnp.dot(weight_v, grid[1], precision=highest, preferred_element_type=jnp.float32)
        block = jnp.stack([jnp.sum(g_real * weight_u, axis=1), jnp.sum(g_imag * weight_u, axis=1)])
        zero = jnp.zeros((), jnp.int32)
        return lax.dynamic_update_slice(
            values, block[:, None, None, :], (zero, jnp.int32(row), jnp.int32(col), offset)
        )

    return lax.fori_loop(jnp.int32(0), turns, step, values)


def per_device(facets, counts, cells, fracs):
    highest = lax.Precision.HIGHEST
    su_dev = counts.shape[0]
    sv_dev = counts.shape[1]
    local_rows = facets.shape[0]
    local_cols = facets.shape[1]
    row_scale = math.sqrt(2.0 / (local_rows * lax.axis_size(FX)))
    col_scale = math.sqrt(2.0 / (local_cols * lax.axis_size("fy")))
    row_index = lax.axis_index(FX)
    col_index = lax.axis_index("fy")
    my_rows = row_index * local_rows + jnp.arange(local_rows, dtype=jnp.int32)
    count = su_dev * lax.axis_size(FX)
    freqs = jnp.arange(count * SUBGRID, dtype=jnp.int32)
    real_part, imag_part = factor(freqs, my_rows, row_scale)
    table = jnp.stack(
        [
            real_part.reshape(count, SUBGRID, local_rows),
            imag_part.reshape(count, SUBGRID, local_rows),
        ],
        axis=1,
    )
    product = jnp.dot(
        table.reshape(count * 2 * SUBGRID, local_rows),
        facets,
        precision=highest,
        preferred_element_type=jnp.float32,
    )
    partial_sums = summed_rows(product.reshape(count, 2, SUBGRID, local_cols), FX, (1, 0), 0)
    piece = lax.all_gather(partial_sums, "fy", axis=3, tiled=True)
    width = piece.shape[3]
    columns = jnp.arange(width, dtype=jnp.int32)
    term = column_term(
        col_index * sv_dev,
        sv_dev,
        piece[:, 0].reshape(su_dev * SUBGRID, width),
        piece[:, 1].reshape(su_dev * SUBGRID, width),
        columns,
        col_scale,
    )
    blank = jnp.zeros((2, su_dev, sv_dev, cells.shape[3]), jnp.float32)
    values = blank
    grid = term[0, :, :, 0:SUBGRID]
    values = degrid(values, grid, cells[:, 0, 0], fracs[:, 0, 0], 0, 0, 1, counts[0, 0])
    return values


def solution(mesh):
    torus = Mesh(mesh.devices.reshape(2, 4, mesh.shape["fy"]), ("fx_0", "fx_1", "fy"))
    in_specs = (P(FX, "fy"), P(FX, "fy"), P(None, FX, "fy", None), P(None, FX, "fy", None))
    out_specs = P(None, FX, "fy", None)
    return jax.shard_map(
        per_device, mesh=torus, in_specs=in_specs, out_specs=out_specs, check_vma=False
    )
```

profile of v0, /device:TPU:43, one launch (start us, length us, event | category | flops | bytes accessed | tf_op | source)
XLA Modules:
  0.0 245.5 jit_solution(14438846253240212937)
XLA Ops:
  6.7 37.7 %cosine_multiply_fusion = (f32[2,4,1,256,1024]{4,3,2,1,0:T(8,128)S(1)}, f32[2,4,1,256,1024]{4,3,2,1,0:T(8,128)S(1)}) fusion(f32[1024]{0:T(1024)S(1)} %fusion.104, s32[2,4,256]{2,1,0:T(4,128)S(1)} %get-tuple-element.134, s32[1024]{0:T(1024)S(1)} %iota_add_fusion.1, s32[2,4,256]{2,1,0:T(4,128)S(1)} %get-tuple-element.133), kind=kLoop, calls=%fused_computation.90 | loop fusion | flops 65011712 | bytes 16801792 | tf_op jit(solution)/shard_map/mul | solution.py:47
  44.4 14.9 %fusion.80 = f32[4,2,1,2,256,256]{5,4,3,0,1,2:T(8,128)S(1)} fusion(f32[2,4,1,256,1024]{4,3,2,1,0:T(8,128)S(1)} %get-tuple-element.130, f32[2,4,1,256,1024]{4,3,2,1,0:T(8,128)S(1)} %get-tuple-element.129, f32[1024,256]{1,0:T(8,128)S(1)} %copy-done), kind=kOutput, calls=%fused_computation.110 | convolution fusion | flops 12889096192 | bytes 22020096 | tf_op jit(solution)/shard_map/dot_general | solution.py:123
  59.4 2.4 copy.6
  61.8 47.6 %reduce-scatter.3.cloned.1.call-done = f32[2,1,2,256,256]{4,3,2,0,1:T(8,128)} async-done(((f32[8,1,2,256,256]{4,3,2,0,1:T(8,128)}), f32[2,1,2,256,256]{4,3,2,0,1:T(8,128)}) %reduce-scatter.3.cloned.1.call-update) | async-done | bytes 1048592 | tf_op jit(solution)/shard_map/reduce_scatter | solution.py:22
  109.5 26.7 %reduce-scatter.5.cloned.1.call-done = f32[1,1,2,256,256]{4,3,2,0,1:T(8,128)} async-done(((f32[2,1,2,256,256]{4,3,2,0,1:T(8,128)}), f32[1,1,2,256,256]{4,3,2,0,1:T(8,128)}) %reduce-scatter.5.cloned.1.call-update) | async-done | bytes 524304 | tf_op jit(solution)/shard_map/reduce_scatter | solution.py:22
  136.4 20.3 %cosine_multiply_fusion.1 = (f32[256,4096]{1,0:T(8,128)}, f32[256,4096]{1,0:T(8,128)}) fusion(f32[4096]{0:T(1024)S(1)} %fusion.90, s32[256]{0:T(256)S(1)} %get-tuple-element.135, s32[256]{0:T(256)S(1)} %get-tuple-element.136), kind=kLoop, calls=%fused_computation.106 | loop fusion | flops 32505856 | bytes 8407040 | tf_op jit(solution)/shard_map/mul | solution.py:47
  156.7 34.1 %all-gather.3.cloned.1.call-done = f32[1,1,2,256,4096]{4,3,2,0,1:T(8,128)} async-done(((f32[1,1,2,256,256]{4,3,2,0,1:T(8,128)}), f32[1,1,2,256,4096]{4,3,2,0,1:T(8,128)}) %all-gather.3.cloned.1.call-update) | async-done | bytes 8388624 | tf_op jit(solution)/shard_map/all_gather | solution.py:130
  190.8 4.1 %slice_bitcast_fusion.1 = (f32[256,4096]{1,0:T(8,128)S(1)}, f32[256,4096]{1,0:T(8,128)S(1)}) fusion(f32[1,2,256,4096]{3,2,1,0:T(8,128)} %bitcast.62), kind=kLoop, calls=%fused_computation.104 | loop fusion | bytes 16777216 | tf_op jit(solution)/shard_map/reshape;squeeze | solution.py:136
  195.0 0.5 copy-done.1
  195.5 1.3 copy-done.2
  196.7 14.3 %fusion.64 = f32[512,512]{1,0:T(8,128)S(1)} fusion(f32[256,4096]{1,0:T(8,128)S(1)} %copy-done.2, f32[256,4096]{1,0:T(8,128)S(1)} %copy-done.1, f32[256,4096]{1,0:T(8,128)S(1)} %get-tuple-element.126, f32[256,4096]{1,0:T(8,128)S(1)} %get-tuple-element.125), kind=kOutput, calls=%fused_computation.82 | convolution fusion | flops 12889096192 | bytes 17825792 | tf_op jit(solution)/shard_map/dot_general | solution.py:64
  211.2 27.2 %while.13 = (s32[]{:T(128)}, f32[2,1,1,2048]{3,2,1,0:T(1,128)S(1)}, s32[]{:T(128)}, s32[2,2048]{1,0:T(2,128)S(1)}, f32[2,2048]{1,0:T(2,128)S(1)}, /*index=5*/f32...) while((s32[]{:T(128)}, f32[2,1,1,2048]{3,2,1,0:T(1,128)S(1)}, s32[]{:T(128)}, ...), condition=%wide.region_5.6_spmd, body=%wide.region_2.5_spmd.sunk | while | flops 203030528 | bytes 603295 | solution.py:99
  211.9 0.4 fusion.129
  212.4 0.4 fusion.128
  213.6 0.4 fusion.129
  214.0 0.4 fusion.128
  215.3 0.4 fusion.129
  215.7 0.4 fusion.128
  217.4 0.4 fusion.128
  219.0 0.4 fusion.128
  220.7 0.4 fusion.128
  222.3 0.4 fusion.128
  224.0 0.4 fusion.128
  225.7 0.4 fusion.128
  227.3 0.4 fusion.128
  229.0 0.4 fusion.128
  230.6 0.4 fusion.128
  232.3 0.4 fusion.128
  233.9 0.4 fusion.128
  235.6 0.4 fusion.128
  237.3 0.4 fusion.128
  238.4 0.6 copy-done.5
  (135 shorter events, 7.4 us)
Async XLA Ops:
  6.5 37.9 %copy-start = (f32[1024,256]{1,0:T(8,128)S(1)}, f32[1024,256]{1,0:T(8,128)}, u32[]{:S(2)}) copy-start(f32[1024,256]{1,0:T(8,128)} %param.6) | copy-start | bytes 3145732
  6.5 102.9 %reduce-scatter.3.cloned.1.call-start = ((), (), s32[]{:S(2)}) async-start(), calls=%async_computation.2 | async-start | bytes 5242880 | tf_op jit(solution)/shard_map/reduce_scatter | solution.py:22
  61.7 74.5 %copy-start.3 = (f32[2,1,1,2048]{3,2,1,0:T(1,128)S(1)}, f32[2,1,1,2048]{3,2,1,0:T(1,128)}, u32[]{:S(2)}) copy-start(f32[2,1,1,2048]{3,2,1,0:T(1,128)} %param.9) | copy-start | bytes 49156
  61.7 74.5 %copy-start.4 = (s32[2,1,1,2048]{3,2,1,0:T(1,128)S(1)}, s32[2,1,1,2048]{3,2,1,0:T(1,128)}, u32[]{:S(2)}) copy-start(s32[2,1,1,2048]{3,2,1,0:T(1,128)} %param.8) | copy-start | bytes 49156
  61.8 74.5 %reduce-scatter.5.cloned.1.call-start = ((), (), s32[]{:S(2)}) async-start(), calls=%async_computation.3 | async-start | bytes 1572864 | tf_op jit(solution)/shard_map/reduce_scatter | solution.py:22
  109.5 81.4 %all-gather.3.cloned.1.call-start = ((), (), s32[]{:S(2)}) async-start(), calls=%async_computation.4 | async-start | bytes 8912896 | tf_op jit(solution)/shard_map/all_gather | solution.py:130
  190.8 4.6 %copy-start.1 = (f32[256,4096]{1,0:T(8,128)S(1)}, f32[256,4096]{1,0:T(8,128)}, u32[]{:S(2)}) copy-start(f32[256,4096]{1,0:T(8,128)} %get-tuple-element.131) | copy-start | bytes 12582916
  190.8 5.9 %copy-start.2 = (f32[256,4096]{1,0:T(8,128)S(1)}, f32[256,4096]{1,0:T(8,128)}, u32[]{:S(2)}) copy-start(f32[256,4096]{1,0:T(8,128)} %get-tuple-element.132) | copy-start | bytes 12582916
  238.4 0.6 copy-start.5
Sparse Core Ops, SparseCore 0:
  61.9 47.4 reduce-scatter.2
  111.8 24.3 reduce-scatter.4
  137.9 52.8 all-gather.2
where the time goes:
time: 246 us
  waiting for transfers between devices  108 us (44%)
  other arithmetic  58.5 us (24%)
  matrix products  43.3 us (18%)
  between operations  13.2 us (5%)
  loops' own time  11.9 us (5%)
  local copies, waits for them, and re-layouts  9.97 us (4%)
    reduce_scatter x2, waiting for transfers between devices, sum_in_order(): blocks = lax.psum_scatter(blocks, axes[k], scatter_dimension=0, tiled=True)  74.3 us
    mul x2, other arithmetic, factor(): return (jnp.cos(angle) * window[None, :], -jnp.sin(angle) * window[None, :])  58 us
    all_gather x1, waiting for transfers between devices, per_device(): piece = lax.all_gather(partial_sums, 'fy', axis=3, tiled=True)  34.1 us
    dot_general x1, matrix products, per_device(): jnp.dot(table.reshape(count * 2 * SUBGRID, local_rows), facets, precision...  14.9 us
    dot_general x1, matrix products, column_term(): lax.dot_general(left, right, (((1,), (1,)), ((), ())), precision=lax.Prec...  14.3 us
    another operation x1, loops' own time, degrid(): return lax.fori_loop(jnp.int32(0), turns, step, values)  11.9 us
    dot_general x16, matrix products, step(): jnp.dot(weight_v, grid[1], precision=highest, preferred_element_type=jnp....  7.06 us
    dot_general x16, matrix products, step(): jnp.dot(weight_v, grid[0], precision=highest, preferred_element_type=jnp....  6.98 us
  transfers between devices with their start and end apart: 3, of which 3 were waited for; matrix products, arithmetic and copies ran while one was open for 8% of the time, Pallas kernels for 0%

commit v1 on v0

--- a/solution.py
+++ b/solution.py
@@ -127,7 +127,7 @@
         preferred_element_type=jnp.float32,
     )
     partial_sums = summed_rows(product.reshape(count, 2, SUBGRID, local_cols), FX, (1, 0), 0)
-    piece = lax.all_gather(partial_sums, "fy", axis=3, tiled=True)
+    piece = jnp.concatenate(lax.all_gather(partial_sums, "fy"), axis=3)
     width = piece.shape[3]
     columns = jnp.arange(width, dtype=jnp.int32)
     term = column_term(

time: 246 us -> 254 us (1.033)
  local copies, waits for them, and re-layouts: 9.97 us -> 18.6 us
    all_gather x0 -> x1, local copies, waits for them, and re-layouts: none -> 8.67 us  [per_device(): piece = jnp.concatenate(lax.all_gather(partial_sums, 'fy'), axis=3)]
where the time goes in v1:
time: 254 us
  waiting for transfers between devices  109 us (43%)
  other arithmetic  58.5 us (23%)
  matrix products  43.1 us (17%)
  local copies, waits for them, and re-layouts  18.6 us (7%)
  between operations  13.3 us (5%)
  loops' own time  11.9 us (5%)
    reduce_scatter x2, waiting for transfers between devices, sum_in_order(): blocks = lax.psum_scatter(blocks, axes[k], scatter_dimension=0, tiled=True)  74.3 us
    mul x2, other arithmetic, factor(): return (jnp.cos(angle) * window[None, :], -jnp.sin(angle) * window[None, :])  58 us
    all_gather x1, waiting for transfers between devices, per_device(): piece = jnp.concatenate(lax.all_gather(partial_sums, 'fy'), axis=3)  34.1 us
    dot_general x1, matrix products, per_device(): jnp.dot(table.reshape(count * 2 * SUBGRID, local_rows), facets, precision...  14.9 us
    dot_general x1, matrix products, column_term(): lax.dot_general(left, right, (((1,), (1,)), ((), ())), precision=lax.Prec...  14.1 us
    another operation x1, loops' own time, degrid(): return lax.fori_loop(jnp.int32(0), turns, step, values)  11.9 us
    all_gather x1, local copies, waits for them, and re-layouts, per_device(): piece = jnp.concatenate(lax.all_gather(partial_sums, 'fy'), axis=3)  8.67 us
    dot_general x16, matrix products, step(): jnp.dot(weight_v, grid[1], precision=highest, preferred_element_type=jnp....  7.06 us
  transfers between devices with their start and end apart: 3, of which 3 were waited for; matrix products, arithmetic and copies ran while one was open for 8% of the time, Pallas kernels for 0%

profile of v1, /device:TPU:43, one launch (start us, length us, event | category | flops | bytes accessed | tf_op | source)
XLA Modules:
  0.0 254.1 jit_solution(16233136711125162758)
XLA Ops:
  6.7 37.7 %cosine_multiply_fusion = (f32[2,4,1,256,1024]{4,3,2,1,0:T(8,128)S(1)}, f32[2,4,1,256,1024]{4,3,2,1,0:T(8,128)S(1)}) fusion(f32[1024]{0:T(1024)S(1)} %fusion.104, s32[2,4,256]{2,1,0:T(4,128)S(1)} %get-tuple-element.134, s32[1024]{0:T(1024)S(1)} %iota_add_fusion.1, s32[2,4,256]{2,1,0:T(4,128)S(1)} %get-tuple-element.133), kind=kLoop, calls=%fused_computation.90 | loop fusion | flops 65011712 | bytes 16801792 | tf_op jit(solution)/shard_map/mul | solution.py:47
  44.4 14.9 %fusion.80 = f32[4,2,1,2,256,256]{5,4,3,0,1,2:T(8,128)S(1)} fusion(f32[2,4,1,256,1024]{4,3,2,1,0:T(8,128)S(1)} %get-tuple-element.130, f32[2,4,1,256,1024]{4,3,2,1,0:T(8,128)S(1)} %get-tuple-element.129, f32[1024,256]{1,0:T(8,128)S(1)} %copy-done), kind=kOutput, calls=%fused_computation.110 | convolution fusion | flops 12889096192 | bytes 22020096 | tf_op jit(solution)/shard_map/dot_general | solution.py:123
  59.4 2.4 copy.9
  61.8 47.6 %reduce-scatter.3.cloned.1.call-done = f32[2,1,2,256,256]{4,3,2,0,1:T(8,128)} async-done(((f32[8,1,2,256,256]{4,3,2,0,1:T(8,128)}), f32[2,1,2,256,256]{4,3,2,0,1:T(8,128)}) %reduce-scatter.3.cloned.1.call-update) | async-done | bytes 1048592 | tf_op jit(solution)/shard_map/reduce_scatter | solution.py:22
  109.5 26.7 %reduce-scatter.5.cloned.1.call-done = f32[1,1,2,256,256]{4,3,2,0,1:T(8,128)} async-done(((f32[2,1,2,256,256]{4,3,2,0,1:T(8,128)}), f32[1,1,2,256,256]{4,3,2,0,1:T(8,128)}) %reduce-scatter.5.cloned.1.call-update) | async-done | bytes 524304 | tf_op jit(solution)/shard_map/reduce_scatter | solution.py:22
  136.4 20.3 %cosine_multiply_fusion.1 = (f32[256,4096]{1,0:T(8,128)}, f32[256,4096]{1,0:T(8,128)}) fusion(f32[4096]{0:T(1024)S(1)} %fusion.90, s32[256]{0:T(256)S(1)} %get-tuple-element.135, s32[256]{0:T(256)S(1)} %get-tuple-element.136), kind=kLoop, calls=%fused_computation.106 | loop fusion | flops 32505856 | bytes 8407040 | tf_op jit(solution)/shard_map/mul | solution.py:47
  156.7 34.1 %all-gather.2.cloned.1.call-done = f32[16,1,2,256,256]{4,3,2,1,0:T(8,128)} async-done(((f32[1,1,2,256,256]{4,3,2,1,0:T(8,128)}), f32[16,1,2,256,256]{4,3,2,1,0:T(8,128)}) %all-gather.2.cloned.1.call-update) | async-done | bytes 8388624 | tf_op jit(solution)/shard_map/all_gather | solution.py:130
  190.9 8.7 %copy.11 = f32[16,1,2,256,256]{3,4,0,2,1:T(8,128)} copy(f32[16,1,2,256,256]{4,3,2,1,0:T(8,128)} %all-gather.2.cloned.1.call-done) | data formatting | bytes 16777216 | tf_op jit(solution)/shard_map/all_gather | solution.py:130
  199.5 4.2 %slice_bitcast_fusion.1 = (f32[256,4096]{0,1:T(8,128)S(1)}, f32[256,4096]{0,1:T(8,128)S(1)}) fusion(f32[1,2,256,4096]{2,3,1,0:T(8,128)} %bitcast.64), kind=kLoop, calls=%fused_computation.104 | loop fusion | bytes 16777216 | tf_op jit(solution)/shard_map/reshape;squeeze | solution.py:136
  203.7 0.5 copy-done.1
  204.2 1.3 copy-done.2
  205.4 14.1 %fusion.64 = f32[512,512]{1,0:T(8,128)S(1)} fusion(f32[256,4096]{1,0:T(8,128)S(1)} %copy-done.2, f32[256,4096]{1,0:T(8,128)S(1)} %copy-done.1, f32[256,4096]{0,1:T(8,128)S(1)} %get-tuple-element.126, f32[256,4096]{0,1:T(8,128)S(1)} %get-tuple-element.125), kind=kOutput, calls=%fused_computation.82 | convolution fusion | flops 12889096192 | bytes 17825792 | tf_op jit(solution)/shard_map/dot_general | solution.py:64
  219.7 27.2 %while.13 = (s32[]{:T(128)}, f32[2,1,1,2048]{3,2,1,0:T(1,128)S(1)}, s32[]{:T(128)}, s32[2,2048]{1,0:T(2,128)S(1)}, f32[2,2048]{1,0:T(2,128)S(1)}, /*index=5*/f32...) while((s32[]{:T(128)}, f32[2,1,1,2048]{3,2,1,0:T(1,128)S(1)}, s32[]{:T(128)}, ...), condition=%wide.region_5.6_spmd, body=%wide.region_2.5_spmd.sunk | while | flops 203030528 | bytes 603295 | solution.py:99
  220.5 0.4 fusion.129
  220.9 0.4 fusion.128
  222.1 0.4 fusion.129
  222.6 0.4 fusion.128
  224.2 0.4 fusion.128
  225.9 0.4 fusion.128
  227.5 0.4 fusion.128
  229.2 0.4 fusion.128
  230.9 0.4 fusion.128
  232.5 0.4 fusion.128
  234.2 0.4 fusion.128
  235.8 0.4 fusion.128
  237.5 0.4 fusion.128
  239.2 0.4 fusion.128
  240.8 0.4 fusion.128
  242.5 0.4 fusion.128
  244.1 0.4 fusion.128
  245.8 0.4 fusion.128
  246.9 0.6 copy-done.5
  (136 shorter events, 7.8 us)
Async XLA Ops:
  6.5 37.9 %copy-start = (f32[1024,256]{1,0:T(8,128)S(1)}, f32[1024,256]{1,0:T(8,128)}, u32[]{:S(2)}) copy-start(f32[1024,256]{1,0:T(8,128)} %param.6) | copy-start | bytes 3145732
  6.5 102.9 %reduce-scatter.3.cloned.1.call-start = ((), (), s32[]{:S(2)}) async-start(), calls=%async_computation.2 | async-start | bytes 5242880 | tf_op jit(solution)/shard_map/reduce_scatter | solution.py:22
  61.7 74.5 %copy-start.3 = (f32[2,1,1,2048]{3,2,1,0:T(1,128)S(1)}, f32[2,1,1,2048]{3,2,1,0:T(1,128)}, u32[]{:S(2)}) copy-start(f32[2,1,1,2048]{3,2,1,0:T(1,128)} %param.9) | copy-start | bytes 49156
  61.7 74.5 %copy-start.4 = (s32[2,1,1,2048]{3,2,1,0:T(1,128)S(1)}, s32[2,1,1,2048]{3,2,1,0:T(1,128)}, u32[]{:S(2)}) copy-start(s32[2,1,1,2048]{3,2,1,0:T(1,128)} %param.8) | copy-start | bytes 49156
  61.8 74.5 %reduce-scatter.5.cloned.1.call-start = ((), (), s32[]{:S(2)}) async-start(), calls=%async_computation.3 | async-start | bytes 1572864 | tf_op jit(solution)/shard_map/reduce_scatter | solution.py:22
  109.5 81.4 %all-gather.2.cloned.1.call-start = ((), (), s32[]{:S(2)}) async-start(), calls=%async_computation.4 | async-start | bytes 8912896 | tf_op jit(solution)/shard_map/all_gather | solution.py:130
  199.5 4.6 %copy-start.1 = (f32[256,4096]{1,0:T(8,128)S(1)}, f32[256,4096]{1,0:T(8,128)}, u32[]{:S(2)}) copy-start(f32[256,4096]{1,0:T(8,128)} %get-tuple-element.131) | copy-start | bytes 12582916
  199.5 5.9 %copy-start.2 = (f32[256,4096]{1,0:T(8,128)S(1)}, f32[256,4096]{1,0:T(8,128)}, u32[]{:S(2)}) copy-start(f32[256,4096]{1,0:T(8,128)} %get-tuple-element.132) | copy-start | bytes 12582916
  246.9 0.6 copy-start.5
Sparse Core Ops, SparseCore 0:
  61.9 47.4 reduce-scatter.2
  111.8 24.3 reduce-scatter.4
  137.9 52.8 all-gather.1
